TPU v7x, 32 devices: a whole 2x2x4 slice. The times are simulated.
32 devices in a mesh: freq: 4 (over x, core), space: 8 (over z, y).
Axes of the slice: x: 2, y: 2, z: 4, core: 2. Of those that a mesh axis runs over, the one named last changes fastest.
Arguments:
- source_field: bfloat16 [2, 8, 1024, 1024], P(None, 'freq', 'space'), may hold values from -6 to 6
- receiver_field: bfloat16 [2, 8, 1024, 1024], P(None, 'freq', 'space'), may hold values from -6 to 6
- line_inverse: bfloat16 [2, 8, 1024, 1024], P(None, 'freq'), may hold values from -0.125 to 0.125
- lens_delay: float32 [3, 1024, 1024], P(None, 'space'), may hold values from -0.6 to 0.6
- omegas: float32 [8], P('freq'), may hold values from 4 to 40
- image_weights: float32 [8], P('freq'), may hold values from 0.1 to 1
Outputs:
- source_out: bfloat16 [2, 8, 1024, 1024], P(None, 'freq', 'space')
- receiver_out: bfloat16 [2, 8, 1024, 1024], P(None, 'freq', 'space')
- gradient: float32 [3, 1024, 1024], P(None, 'space')
All inputs are finite; a program needn't handle non-finite values.
Results may differ from a plain program's by a relative error of at most 0.017.
Values may be sent and summed in bfloat16 or wider, within the bound.
No kernel may reach another device: no remote copies, remote signals or barrier semaphores. Data moves between devices by JAX's collectives and lax.ppermute only.
A program may use at most 128 MiB of HBM per device.

v0:
```python
import jax
import jax.numpy as jnp
from jax import lax
from jax.sharding import PartitionSpec as P


def to_blocks(matrix, pieces):
    leading = matrix.shape[:-2]
    local_rows = matrix.shape[-2]
    columns = matrix.shape[-1] // pieces
    arranged = matrix.reshape(leading + (local_rows, pieces, columns))
    arranged = jnp.moveaxis(arranged, -2, -3)
    return arranged.reshape(leading + (pieces, local_rows * columns))


def from_blocks(blocked, local_rows):
    leading = blocked.shape[:-2]
    pieces = blocked.shape[-2]
    columns = blocked.shape[-1] // local_rows
    arranged = blocked.reshape(leading + (pieces, local_rows, columns))
    arranged = jnp.moveaxis(arranged, -1, -3)
    return arranged.reshape(leading + (columns, pieces * local_rows))


def rotate(fields, phase_angle):
    cosine = jnp.cos(phase_angle)
    sine_part = jnp.sin(phase_angle)
    flip_sign = jnp.array([1.0, -1.0], jnp.float32).reshape(2, 1, 1, 1)
    real_part = fields[:, 0]
    imag_part = fields[:, 1]
    return jnp.stack(
        [
            real_part * cosine + flip_sign * imag_part * sine_part,
            imag_part * cosine - flip_sign * real_part * sine_part,
        ],
        axis=1,
    )


def line_solve(line_inverse, fields):
    flip_sign = jnp.array([1.0, -1.0], jnp.float32).reshape(2, 1, 1, 1)
    prod_real = jnp.einsum(
        "fij,wpfrj->wpfri", line_inverse[0], fields, preferred_element_type=jnp.float32
    )
    prod_imag = jnp.einsum(
        "fij,wpfrj->wpfri", line_inverse[1], fields, preferred_element_type=jnp.float32
    )
    new_real = prod_real[:, 0] - flip_sign * prod_imag[:, 1]
    new_imag = prod_real[:, 1] + flip_sign * prod_imag[:, 0]
    return jnp.stack([new_real, new_imag], axis=1)


def march_step(line_inverse, phased, local_rows):
    pieces = lax.axis_size("space")
    across = line_solve(line_inverse, phased).astype(jnp.bfloat16)
    received = lax.all_to_all(
        to_blocks(across, pieces), "space", split_axis=3, concat_axis=3, tiled=True
    )
    return line_solve(line_inverse, from_blocks(received, local_rows))


def image_slice(fields, image_weights):
    image_term = fields[0, 0] * fields[1, 0] + fields[0, 1] * fields[1, 1]
    return jnp.sum(image_weights[:, None, None] * image_term, axis=0)


def reduce_slice(image_term):
    return lax.psum(image_term.astype(jnp.bfloat16), "freq").astype(jnp.float32)


def finish_sums(slices):
    stacked = jnp.stack(slices)
    return stacked


def on_device(source_field, receiver_field, line_inverse, lens_delay, omegas, image_weights):
    pieces = lax.axis_size("space")
    local_rows = lens_delay.shape[1]
    depth_count = lens_delay.shape[0]
    wavefields = jnp.stack([source_field, receiver_field]).astype(jnp.float32)
    slices = []
    lens_columns = from_blocks(
        lax.all_to_all(
            to_blocks(lens_delay, pieces), "space", split_axis=1, concat_axis=1, tiled=True
        ),
        local_rows,
    )
    phased = rotate(wavefields, omegas[:, None, None] * lens_delay[0][None]).astype(jnp.bfloat16)
    solved = march_step(line_inverse, phased, local_rows)
    slices.append(reduce_slice(image_slice(solved, image_weights)))
    for depth_step in range(1, depth_count):
        phase_angle = omegas[:, None, None] * lens_columns[depth_step][None]
        phased_columns = rotate(solved, phase_angle).astype(jnp.bfloat16)
        received = lax.all_to_all(
            to_blocks(phased_columns, pieces), "space", split_axis=3, concat_axis=3, tiled=True
        )
        solved = march_step(line_inverse, from_blocks(received, local_rows), local_rows)
        slices.append(reduce_slice(image_slice(solved, image_weights)))
    final_blocks = lax.all_to_all(
        to_blocks(solved.astype(jnp.bfloat16), pieces),
        "space",
        split_axis=3,
        concat_axis=3,
        tiled=True,
    )
    final_fields = from_blocks(final_blocks, local_rows)
    gradient_columns = finish_sums(slices)
    gradient = from_blocks(
        lax.all_to_all(
            to_blocks(gradient_columns, pieces).astype(jnp.bfloat16),
            "space",
            split_axis=1,
            concat_axis=1,
            tiled=True,
        ).astype(jnp.float32),
        local_rows,
    )
    return (final_fields[0], final_fields[1], gradient)


def solution(mesh):
    placed = (
        P(None, "freq", "space", None),
        P(None, "freq", "space", None),
        P(None, "freq", None, None),
        P(None, "space", None),
        P("freq"),
        P("freq"),
    )
    return jax.shard_map(
        on_device,
        mesh=mesh,
        in_specs=placed,
        out_specs=(
            P(None, "freq", "space", None),
            P(None, "freq", "space", None),
            P(None, "space", None),
        ),
        check_vma=False,
    )
```

profile of v0, /device:TPU:0, one launch (start us, length us, event | category | flops | bytes accessed | tf_op | source)
XLA Modules:
  0.0 648.7 jit_solution(17331599846674338511)
XLA Ops:
  9.1 2.5 copy.277
  11.5 7.4 %all-to-all-start.1 = ((f32[3,8,16384]{2,0,1:T(4,128)}), f32[3,8,16384]{2,0,1:T(4,128)S(1)}, u32[]{:S(2)}, u32[]{:S(2)}) async-start(f32[3,8,16384]{2,0,1:T(4,128)} %copy.277), calls=%async_computation.1 | async-start | bytes 4194304 | tf_op jit(solution)/shard_map/all_to_all | solution.py:83
  20.4 2.2 maximum_convert_fusion
  22.6 1.9 slice_bitcast_fusion
  24.5 42.7 %all-to-all-done.1 = f32[3,8,16384]{2,0,1:T(4,128)S(1)} async-done(((f32[3,8,16384]{2,0,1:T(4,128)}), f32[3,8,16384]{2,0,1:T(4,128)S(1)}, u32[]{:S(2)}, u32[]{:S(2)}) %all-to-all-start.1) | async-done | bytes 1572896 | tf_op jit(solution)/shard_map/all_to_all | solution.py:83
  67.2 2.1 reshape.222
  71.8 12.3 %multiply_cosine_fusion.2 = (f32[2,128,1024]{2,1,0:T(8,128)S(1)}, f32[2,128,1024]{2,1,0:T(8,128)S(1)}, f32[2,128,1024]{2,1,0:T(8,128)}, f32[2,128,1024]{2,1,0:T(...) fusion(f32[128,1024]{1,0:T(8,128)S(1)} %copy-done.20, f32[2]{0:T(128)S(1)} %copy-done.28, ...), kind=kLoop, calls=%fused_computation.110 | loop fusion | flops 786432 | bytes 7864328 | tf_op jit(solution)/shard_map/cos | solution.py:26
  85.2 4.7 fusion.33
  90.0 2.4 fusion.51
  94.9 2.8 reshape.190
  97.7 3.7 copy.270
  101.4 51.8 %all_to_all.40 = bf16[2,2,2,8,16384]{4,2,1,0,3:T(2,128)(2,1)S(1)} all-to-all(bf16[2,2,2,8,16384]{4,2,1,0,3:T(2,128)(2,1)S(1)} %copy.270), channel_id=1, replica_groups=mesh['freq'=4,'space'=8] {'space'}, dimensions={3} | all-to-all | bytes 4194304 | tf_op jit(solution)/shard_map/all_to_all | solution.py:56
  153.3 2.8 reshape.220
  156.1 3.1 copy.343
  159.2 2.3 reshape.221
  161.5 5.3 fusion.27
  166.9 6.1 fusion.45
  176.6 2.3 reshape.196
  178.9 3.7 copy.285
  182.7 51.6 %all_to_all.41 = bf16[2,2,2,8,16384]{4,2,1,0,3:T(2,128)(2,1)S(1)} all-to-all(bf16[2,2,2,8,16384]{4,2,1,0,3:T(2,128)(2,1)S(1)} %copy.285), channel_id=1, replica_groups=mesh['freq'=4,'space'=8] {'space'}, dimensions={3} | all-to-all | bytes 4194304 | tf_op jit(solution)/shard_map/all_to_all | solution.py:94
  234.2 2.8 reshape.223
  237.1 3.1 copy.287
  240.1 2.3 reshape.198
  242.5 5.3 fusion.36
  247.8 4.6 fusion.54
  254.9 2.3 reshape.199
  257.2 3.7 copy.290
  261.0 51.4 %all_to_all.42 = bf16[2,2,2,8,16384]{4,2,1,0,3:T(2,128)(2,1)S(1)} all-to-all(bf16[2,2,2,8,16384]{4,2,1,0,3:T(2,128)(2,1)S(1)} %copy.290), channel_id=1, replica_groups=mesh['freq'=4,'space'=8] {'space'}, dimensions={3} | all-to-all | bytes 4194304 | tf_op jit(solution)/shard_map/all_to_all | solution.py:56
  312.4 2.8 reshape.224
  315.2 3.1 copy.350
  318.3 2.3 reshape.225
  320.6 5.3 fusion.30
  326.0 6.1 fusion.48
  335.6 2.3 reshape.202
  338.0 3.7 copy.302
  341.7 51.6 %all_to_all.43 = bf16[2,2,2,8,16384]{4,2,1,0,3:T(2,128)(2,1)S(1)} all-to-all(bf16[2,2,2,8,16384]{4,2,1,0,3:T(2,128)(2,1)S(1)} %copy.302), channel_id=1, replica_groups=mesh['freq'=4,'space'=8] {'space'}, dimensions={3} | all-to-all | bytes 4194304 | tf_op jit(solution)/shard_map/all_to_all | solution.py:94
  393.3 2.8 reshape.226
  396.1 3.1 copy.304
  399.2 2.3 reshape.204
  401.6 5.3 fusion.39
  406.9 4.6 fusion.57
  414.0 2.3 reshape.205
  416.3 3.7 copy.307
  420.1 51.4 %all_to_all.44 = bf16[2,2,2,8,16384]{4,2,1,0,3:T(2,128)(2,1)S(1)} all-to-all(bf16[2,2,2,8,16384]{4,2,1,0,3:T(2,128)(2,1)S(1)} %copy.307), channel_id=1, replica_groups=mesh['freq'=4,'space'=8] {'space'}, dimensions={3} | all-to-all | bytes 4194304 | tf_op jit(solution)/shard_map/all_to_all | solution.py:56
  471.5 2.8 reshape.227
  474.3 3.1 copy.356
  477.4 2.3 reshape.228
  479.7 5.3 fusion.24
  485.1 8.1 %fusion.42 = f32[2,2,2,128,1024]{4,3,2,0,1:T(8,128)} fusion(bf16[2,2,2,128,1024]{4,3,2,0,1:T(8,128)(2,1)S(1)} %copy-done.25, bf16[2,2,1024,1024]{3,2,1,0:T(8,128)(2,1)} %param.17), kind=kOutput, calls=%fused_computation.30 | convolution fusion | flops 2147483648 | bytes 10485760 | tf_op jit(solution)/shard_map/fij,wpfrj->wpfri/dot_general | solution.py:42
  493.2 6.4 fusion.72
  499.7 6.2 subtract_convert_fusion
  508.7 1.6 fusion.103
  512.9 34.0 %all-reduce.3.cloned.1.call-done = (bf16[1,128,8,128]{1,3,2,0:T(8,128)(2,1)}, bf16[1,128,8,128]{1,3,2,0:T(8,128)(2,1)}, bf16[1,128,8,128]{1,3,2,0:T(8,128)(2,1)}) async-done(((bf16[1,128,8,128]{1,3,2,0:T(8,128)(2,1)}, bf16[1,128,8,128]{1,3,2,0:T(8,128)(2,1)}, bf16[1,128,8,128]{1,3,2,0:T(8,128)(2,1)}), (bf16[1,128,8,128]{1,3,2,0:T(8,128)(2,1)}, bf16[1,128,8,128]{1,3,2,0:T(8,128)(2,1)}, ...) | async-done | bytes 786448 | tf_op jit(solution)/shard_map/psum | solution.py:68
  546.9 2.1 maximum_bitcast_fusion.6
  551.6 5.8 all-to-all-start.7
  557.4 1.6 copy.373
  560.6 2.3 reshape.208
  562.9 5.1 copy.317
  568.0 14.5 %all-to-all-done.7 = bf16[3,8,16384]{2,0,1:T(4,128)(2,1)S(1)} async-done(((bf16[3,8,16384]{2,0,1:T(4,128)(2,1)}), bf16[3,8,16384]{2,0,1:T(4,128)(2,1)S(1)}, u32[]{:S(2)}, u32[]{:S(2)}) %all-to-all-start.7) | async-done | bytes 786464 | tf_op jit(solution)/shard_map/all_to_all | solution.py:109
  582.5 3.6 all-to-all-start.6
  588.2 3.0 copy.329
  591.2 43.1 %all-to-all-done.6 = bf16[2,2,2,8,16384]{4,2,1,0,3:T(2,128)(2,1)S(1)} async-done(((bf16[2,2,2,8,16384]{4,2,1,0,3:T(2,128)(2,1)}), bf16[2,2,2,8,16384]{4,2,1,0,3:T(2,128)(2,1)S(1)}, u32[]{:S(2)}, u32[]{:S(2)}) %all-to-all-start.6) | async-done | bytes 2097184 | tf_op jit(solution)/shard_map/all_to_all | solution.py:99
  634.3 2.8 reshape.229
  637.1 1.7 copy.391
  (121 shorter events, 35.6 us)
Async XLA Ops:
  11.5 7.5 %copy-start.26 = (bf16[2,2,128,1024]{3,2,1,0:T(8,128)(2,1)S(1)}, bf16[2,2,128,1024]{3,2,1,0:T(8,128)(2,1)}, u32[]{:S(2)}) copy-start(bf16[2,2,128,1024]{3,2,1,0:T(8,128)(2,1)} %param.16) | copy-start | bytes 3145732
  11.5 55.7 %all-to-all-start.1 = ((f32[3,8,16384]{2,0,1:T(4,128)}), f32[3,8,16384]{2,0,1:T(4,128)S(1)}, u32[]{:S(2)}, u32[]{:S(2)}) async-start(f32[3,8,16384]{2,0,1:T(4,128)} %copy.277), calls=%async_computation.1 | async-start | bytes 4194304 | tf_op jit(solution)/shard_map/all_to_all | solution.py:83
  18.9 528.0 %all-reduce.3.cloned.1.call-start = ((), (), s32[]{:S(2)}) async-start(), calls=%async_computation.8 | async-start | bytes 1572864 | tf_op jit(solution)/shard_map/psum | solution.py:68
  70.8 1.0 copy-start.20
  70.8 1.0 copy-start.28
  71.8 12.3 %copy-start.8 = (f32[2,2,2,128,1024]{4,3,1,0,2:T(8,128)S(1)}, f32[2,2,2,128,1024]{4,3,1,0,2:T(8,128)}, u32[]{:S(2)}) copy-start(f32[2,2,2,128,1024]{4,3,1,0,2:T(8,128)} %maximum_convert_fusion) | copy-start | bytes 12582916
  71.8 12.3 %copy-start.27 = (f32[2]{0:T(128)S(1)}, f32[2]{0:T(128)}, u32[]{:S(2)}) copy-start(f32[2]{0:T(128)} %constant.4.clone) | copy-start | bytes 28
  84.2 5.8 slice-start
  85.2 4.8 slice-start.1
  161.5 5.3 copy-start.21
  166.8 6.2 copy-start
  166.9 6.2 copy-start.18
  166.9 6.2 copy-start.19
  173.0 2.3 copy-start.2
  242.5 5.3 copy-start.22
  320.6 5.3 copy-start.23
  326.0 6.1 copy-start.4
  326.0 6.1 copy-start.17
  332.1 2.3 copy-start.6
  401.6 5.3 copy-start.24
  479.7 5.3 copy-start.25
  479.7 13.5 %copy-start.7 = (f32[2,2,2,128,1024]{4,3,2,0,1:T(8,128)S(1)}, f32[2,2,2,128,1024]{4,3,2,0,1:T(8,128)}, u32[]{:S(2)}) copy-start(f32[2,2,2,128,1024]{4,3,2,0,1:T(8,128)} %copy-done.6) | copy-start | bytes 12582916
  485.1 8.2 %copy-start.9 = (f32[2,2,2,128,1024]{4,3,2,0,1:T(8,128)}, f32[2,2,2,128,1024]{4,3,2,0,1:T(8,128)S(1)}, u32[]{:S(2)}) copy-start(f32[2,2,2,128,1024]{4,3,2,0,1:T(8,128)S(1)} %fusion.24) | copy-start | bytes 12582916
  485.1 8.2 %copy-start.1 = (f32[2,2,2,128,1024]{4,3,2,0,1:T(8,128)S(1)}, f32[2,2,2,128,1024]{4,3,2,0,1:T(8,128)}, u32[]{:S(2)}) copy-start(f32[2,2,2,128,1024]{4,3,2,0,1:T(8,128)} %copy-done) | copy-start | bytes 12582916
  485.1 8.2 %copy-start.3 = (f32[2,2,2,128,1024]{4,3,2,0,1:T(8,128)S(1)}, f32[2,2,2,128,1024]{4,3,2,0,1:T(8,128)}, u32[]{:S(2)}) copy-start(f32[2,2,2,128,1024]{4,3,2,0,1:T(8,128)} %copy-done.2) | copy-start | bytes 12582916
  485.1 8.2 %copy-start.5 = (f32[2,2,2,128,1024]{4,3,2,0,1:T(8,128)S(1)}, f32[2,2,2,128,1024]{4,3,2,0,1:T(8,128)}, u32[]{:S(2)}) copy-start(f32[2,2,2,128,1024]{4,3,2,0,1:T(8,128)} %copy-done.4) | copy-start | bytes 12582916
  499.6 6.2 copy-start.10
  499.6 6.7 %copy-start.14 = (f32[2,2,128,1024]{3,2,1,0:T(8,128)S(1)}, f32[2,2,128,1024]{3,2,1,0:T(8,128)}, u32[]{:S(2)}) copy-start(f32[2,2,128,1024]{3,2,1,0:T(8,128)} %get-tuple-element.57) | copy-start | bytes 6291460
  499.7 6.7 %copy-start.15 = (f32[2,2,128,1024]{3,2,1,0:T(8,128)S(1)}, f32[2,2,128,1024]{3,2,1,0:T(8,128)}, u32[]{:S(2)}) copy-start(f32[2,2,128,1024]{3,2,1,0:T(8,128)} %get-tuple-element.58) | copy-start | bytes 6291460
  505.9 1.6 copy-start.11
  505.9 2.2 copy-start.12
  505.9 2.9 copy-start.13
  505.9 2.8 copy-start.29
  551.6 30.8 %all-to-all-start.7 = ((bf16[3,8,16384]{2,0,1:T(4,128)(2,1)}), bf16[3,8,16384]{2,0,1:T(4,128)(2,1)S(1)}, u32[]{:S(2)}, u32[]{:S(2)}) async-start(bf16[3,8,16384]{2,0,1:T(4,128)(2,1)} %reshape.230), calls=%async_computation.7 | async-start | bytes 2097152 | tf_op jit(solution)/shard_map/all_to_all | solution.py:109
  557.4 1.9 copy-start.16
  582.5 51.8 %all-to-all-start.6 = ((bf16[2,2,2,8,16384]{4,2,1,0,3:T(2,128)(2,1)}), bf16[2,2,2,8,16384]{4,2,1,0,3:T(2,128)(2,1)S(1)}, u32[]{:S(2)}, u32[]{:S(2)}) async-start(bf16[2,2,2,8,16384]{4,2,1,0,3:T(2,128)(2,1)} %copy.317), calls=%async_computation.6 | async-start | bytes 4194304 | tf_op jit(solution)/shard_map/all_to_all | solution.py:99
Sparse Core Ops, SparseCore 0:
  513.0 33.8 all-reduce.2
where the time goes:
time: 659 us; the launch traced here: 649 us
  blocking collectives  258 us (39%)
  waiting for transfers between devices  134 us (20%)
  local copies, waits for them, and re-layouts  120 us (18%)
  matrix products  63.2 us (10%)
  other arithmetic  41.5 us (6%)
  starting transfers between devices  16.8 us (3%)
  between operations  15.1 us (2%)
    all_to_all x3, blocking collectives, march_step(): lax.all_to_all(to_blocks(across, pieces), 'space', split_axis=3, concat_a...  155 us
    all_to_all x2, blocking collectives, on_device(): lax.all_to_all(to_blocks(phased_columns, pieces), 'space', split_axis=3,...  103 us
    all_to_all x1, waiting for transfers between devices, on_device(): lax.all_to_all(to_blocks(solved.astype(jnp.bfloat16), pieces), 'space', s...  43.1 us
    all_to_all x1, waiting for transfers between devices, on_device(): lax.all_to_all(to_blocks(lens_delay, pieces), 'space', split_axis=1, conc...  42.7 us
    reshape x14, local copies, waits for them, and re-layouts, to_blocks(): return arranged.reshape(leading + (pieces, local_rows * columns))  41 us
    psum x1, waiting for transfers between devices, reduce_slice(): return lax.psum(image_term.astype(jnp.bfloat16), 'freq').astype(jnp.float32)  34 us
    dot_general x6, matrix products, line_solve(): jnp.einsum('fij,wpfrj->wpfri', line_inverse[0], fields, preferred_element...  31.8 us
    dot_general x6, matrix products, line_solve(): jnp.einsum('fij,wpfrj->wpfri', line_inverse[1], fields, preferred_element...  31.4 us
  transfers between devices with their start and end apart: 4, of which 4 were waited for; matrix products, arithmetic and copies ran while one was open for 3% of the time, Pallas kernels for 0%

commit v1 on v0

--- a/solution.py
+++ b/solution.py
@@ -65,7 +65,9 @@
 
 
 def reduce_slice(image_term):
-    return lax.psum(image_term.astype(jnp.bfloat16), "freq").astype(jnp.float32)
+    return jnp.sum(lax.all_gather(image_term.astype(jnp.bfloat16), "freq"), axis=0).astype(
+        jnp.float32
+    )
 
 
 def finish_sums(slices):

time: 659 us -> 678 us (1.029)
  waiting for transfers between devices: 134 us -> 151 us
    all_gather x0 -> x3, waiting for transfers between devices: none -> 48.2 us  [reduce_slice(): lax.all_gather(image_term.astype(jnp.bfloat16), 'freq')]
    psum x1 -> x0, waiting for transfers between devices: 34 us -> none  [reduce_slice(): return lax.psum(image_term.astype(jnp.bfloat16), 'freq').astype(jnp.float32)]
  transfers between devices with their start and end apart: 4 -> 6, of which waited for: 4 -> 6; matrix products, arithmetic and copies ran while one was open for 3% -> 4% of each run, Pallas kernels for 0% -> 0%
where the time goes in v1:
time: 678 us; the launch traced here: 667 us
  blocking collectives  258 us (38%)
  waiting for transfers between devices  151 us (22%)
  local copies, waits for them, and re-layouts  118 us (17%)
  matrix products  63.2 us (9%)
  other arithmetic  45.7 us (7%)
  starting transfers between devices  17 us (3%)
  between operations  14.8 us (2%)
    all_to_all x3, blocking collectives, march_step(): lax.all_to_all(to_blocks(across, pieces), 'space', split_axis=3, concat_a...  155 us
    all_to_all x2, blocking collectives, on_device(): lax.all_to_all(to_blocks(phased_columns, pieces), 'space', split_axis=3,...  103 us
    all_gather x3, waiting for transfers between devices, reduce_slice(): lax.all_gather(image_term.astype(jnp.bfloat16), 'freq')  48.2 us
    all_to_all x1, waiting for transfers between devices, on_device(): lax.all_to_all(to_blocks(solved.astype(jnp.bfloat16), pieces), 'space', s...  43.4 us
    all_to_all x1, waiting for transfers between devices, on_device(): lax.all_to_all(to_blocks(lens_delay, pieces), 'space', split_axis=1, conc...  42.7 us
    reshape x14, local copies, waits for them, and re-layouts, to_blocks(): return arranged.reshape(leading + (pieces, local_rows * columns))  41 us
    dot_general x6, matrix products, line_solve(): jnp.einsum('fij,wpfrj->wpfri', line_inverse[0], fields, preferred_element...  31.8 us
    dot_general x6, matrix products, line_solve(): jnp.einsum('fij,wpfrj->wpfri', line_inverse[1], fields, preferred_element...  31.4 us
  transfers between devices with their start and end apart: 6, of which 6 were waited for; matrix products, arithmetic and copies ran while one was open for 4% of the time, Pallas kernels for 0%

profile of v1, /device:TPU:0, one launch (start us, length us, event | category | flops | bytes accessed | tf_op | source)
XLA Modules:
  0.0 667.5 jit_solution(9960343961219125715)
XLA Ops:
  9.1 2.5 copy.277
  11.5 7.4 %all-to-all-start.1 = ((f32[3,8,16384]{2,0,1:T(4,128)}), f32[3,8,16384]{2,0,1:T(4,128)S(1)}, u32[]{:S(2)}, u32[]{:S(2)}) async-start(f32[3,8,16384]{2,0,1:T(4,128)} %copy.277), calls=%async_computation.1 | async-start | bytes 4194304 | tf_op jit(solution)/shard_map/all_to_all | solution.py:85
  20.4 2.2 maximum_convert_fusion
  22.7 1.9 slice_bitcast_fusion
  24.5 42.7 %all-to-all-done.1 = f32[3,8,16384]{2,0,1:T(4,128)S(1)} async-done(((f32[3,8,16384]{2,0,1:T(4,128)}), f32[3,8,16384]{2,0,1:T(4,128)S(1)}, u32[]{:S(2)}, u32[]{:S(2)}) %all-to-all-start.1) | async-done | bytes 1572896 | tf_op jit(solution)/shard_map/all_to_all | solution.py:85
  67.2 2.1 reshape.282
  71.8 12.3 %multiply_cosine_fusion.2 = (f32[2,128,1024]{2,1,0:T(8,128)S(1)}, f32[2,128,1024]{2,1,0:T(8,128)S(1)}, f32[2,128,1024]{2,1,0:T(8,128)}, f32[2,128,1024]{2,1,0:T(...) fusion(f32[128,1024]{1,0:T(8,128)S(1)} %copy-done.20, f32[2]{0:T(128)S(1)} %copy-done.28, ...), kind=kLoop, calls=%fused_computation.110 | loop fusion | flops 786432 | bytes 7864328 | tf_op jit(solution)/shard_map/cos | solution.py:26
  85.3 4.7 fusion.33
  90.0 2.4 fusion.51
  94.9 2.8 reshape.247
  97.7 3.7 copy.270
  101.5 51.8 %all_to_all.40 = bf16[2,2,2,8,16384]{4,2,1,0,3:T(2,128)(2,1)S(1)} all-to-all(bf16[2,2,2,8,16384]{4,2,1,0,3:T(2,128)(2,1)S(1)} %copy.270), channel_id=1, replica_groups=mesh['freq'=4,'space'=8] {'space'}, dimensions={3} | all-to-all | bytes 4194304 | tf_op jit(solution)/shard_map/all_to_all | solution.py:56
  153.3 2.8 reshape.280
  156.1 3.1 copy.343
  159.2 2.3 reshape.281
  161.5 5.3 fusion.27
  166.9 6.1 fusion.45
  176.6 2.3 reshape.253
  178.9 3.7 copy.285
  182.7 51.6 %all_to_all.41 = bf16[2,2,2,8,16384]{4,2,1,0,3:T(2,128)(2,1)S(1)} all-to-all(bf16[2,2,2,8,16384]{4,2,1,0,3:T(2,128)(2,1)S(1)} %copy.285), channel_id=1, replica_groups=mesh['freq'=4,'space'=8] {'space'}, dimensions={3} | all-to-all | bytes 4194304 | tf_op jit(solution)/shard_map/all_to_all | solution.py:96
  234.3 2.8 reshape.283
  237.1 3.1 copy.287
  240.2 2.3 reshape.255
  242.5 5.3 fusion.36
  247.8 4.6 fusion.54
  254.9 2.3 reshape.256
  257.3 3.7 copy.290
  261.0 51.4 %all_to_all.42 = bf16[2,2,2,8,16384]{4,2,1,0,3:T(2,128)(2,1)S(1)} all-to-all(bf16[2,2,2,8,16384]{4,2,1,0,3:T(2,128)(2,1)S(1)} %copy.290), channel_id=1, replica_groups=mesh['freq'=4,'space'=8] {'space'}, dimensions={3} | all-to-all | bytes 4194304 | tf_op jit(solution)/shard_map/all_to_all | solution.py:56
  312.4 2.8 reshape.284
  315.2 3.1 copy.350
  318.3 2.3 reshape.285
  320.7 5.3 fusion.30
  326.0 6.1 fusion.48
  335.7 2.3 reshape.259
  338.0 3.7 copy.302
  341.7 51.6 %all_to_all.43 = bf16[2,2,2,8,16384]{4,2,1,0,3:T(2,128)(2,1)S(1)} all-to-all(bf16[2,2,2,8,16384]{4,2,1,0,3:T(2,128)(2,1)S(1)} %copy.302), channel_id=1, replica_groups=mesh['freq'=4,'space'=8] {'space'}, dimensions={3} | all-to-all | bytes 4194304 | tf_op jit(solution)/shard_map/all_to_all | solution.py:96
  393.3 2.8 reshape.286
  396.1 3.1 copy.304
  399.2 2.3 reshape.261
  401.6 5.3 fusion.39
  406.9 4.6 fusion.57
  414.0 2.3 reshape.262
  416.3 3.7 copy.307
  420.1 51.4 %all_to_all.44 = bf16[2,2,2,8,16384]{4,2,1,0,3:T(2,128)(2,1)S(1)} all-to-all(bf16[2,2,2,8,16384]{4,2,1,0,3:T(2,128)(2,1)S(1)} %copy.307), channel_id=1, replica_groups=mesh['freq'=4,'space'=8] {'space'}, dimensions={3} | all-to-all | bytes 4194304 | tf_op jit(solution)/shard_map/all_to_all | solution.py:56
  471.4 2.8 reshape.287
  474.2 3.1 copy.356
  477.3 2.3 reshape.288
  479.6 5.3 fusion.24
  485.0 8.1 %fusion.42 = f32[2,2,2,128,1024]{4,3,2,0,1:T(8,128)} fusion(bf16[2,2,2,128,1024]{4,3,2,0,1:T(8,128)(2,1)S(1)} %copy-done.25, bf16[2,2,1024,1024]{3,2,1,0:T(8,128)(2,1)} %param.17), kind=kOutput, calls=%fused_computation.30 | convolution fusion | flops 2147483648 | bytes 10485760 | tf_op jit(solution)/shard_map/fij,wpfrj->wpfri/dot_general | solution.py:42
  493.2 6.4 fusion.72
  499.7 6.2 subtract_convert_fusion
  508.7 2.6 fusion.103
  512.8 14.3 %all-gather.7.cloned.1.call-done = bf16[512,1024]{1,0:T(8,128)(2,1)} async-done(((bf16[128,1024]{1,0:T(8,128)(2,1)}), bf16[512,1024]{1,0:T(8,128)(2,1)}) %all-gather.7.cloned.1.call-update) | async-done | bytes 1048592 | tf_op jit(solution)/shard_map/all_gather | solution.py:68
  528.7 17.3 %all-gather.9.cloned.1.call-done = bf16[512,1024]{1,0:T(8,128)(2,1)} async-done(((bf16[128,1024]{1,0:T(8,128)(2,1)}), bf16[512,1024]{1,0:T(8,128)(2,1)}) %all-gather.9.cloned.1.call-update) | async-done | bytes 1048592 | tf_op jit(solution)/shard_map/all_gather | solution.py:68
  547.6 16.7 %all-gather.11.cloned.1.call-done = bf16[512,1024]{1,0:T(8,128)(2,1)} async-done(((bf16[128,1024]{1,0:T(8,128)(2,1)}), bf16[512,1024]{1,0:T(8,128)(2,1)}) %all-gather.11.cloned.1.call-update) | async-done | bytes 1048592 | tf_op jit(solution)/shard_map/all_gather | solution.py:68
  569.5 5.8 all-to-all-start.7
  578.4 2.3 reshape.265
  580.8 5.1 copy.317
  585.9 15.5 %all-to-all-done.7 = bf16[3,8,16384]{2,0,1:T(4,128)(2,1)S(1)} async-done(((bf16[3,8,16384]{2,0,1:T(4,128)(2,1)}), bf16[3,8,16384]{2,0,1:T(4,128)(2,1)S(1)}, u32[]{:S(2)}, u32[]{:S(2)}) %all-to-all-start.7) | async-done | bytes 786464 | tf_op jit(solution)/shard_map/all_to_all | solution.py:111
  601.4 3.6 all-to-all-start.6
  607.0 3.0 copy.329
  610.1 43.4 %all-to-all-done.6 = bf16[2,2,2,8,16384]{4,2,1,0,3:T(2,128)(2,1)S(1)} async-done(((bf16[2,2,2,8,16384]{4,2,1,0,3:T(2,128)(2,1)}), bf16[2,2,2,8,16384]{4,2,1,0,3:T(2,128)(2,1)S(1)}, u32[]{:S(2)}, u32[]{:S(2)}) %all-to-all-start.6) | async-done | bytes 2097184 | tf_op jit(solution)/shard_map/all_to_all | solution.py:101
  653.4 2.8 reshape.289
  656.2 1.7 copy.391
  (130 shorter events, 41.9 us)
Async XLA Ops:
  11.5 7.5 %copy-start.26 = (bf16[2,2,128,1024]{3,2,1,0:T(8,128)(2,1)S(1)}, bf16[2,2,128,1024]{3,2,1,0:T(8,128)(2,1)}, u32[]{:S(2)}) copy-start(bf16[2,2,128,1024]{3,2,1,0:T(8,128)(2,1)} %param.16) | copy-start | bytes 3145732
  11.5 55.7 %all-to-all-start.1 = ((f32[3,8,16384]{2,0,1:T(4,128)}), f32[3,8,16384]{2,0,1:T(4,128)S(1)}, u32[]{:S(2)}, u32[]{:S(2)}) async-start(f32[3,8,16384]{2,0,1:T(4,128)} %copy.277), calls=%async_computation.1 | async-start | bytes 4194304 | tf_op jit(solution)/shard_map/all_to_all | solution.py:85
  19.0 508.2 %all-gather.7.cloned.1.call-start = ((), (), s32[]{:S(2)}) async-start(), calls=%async_computation.8 | async-start | bytes 1310720 | tf_op jit(solution)/shard_map/all_gather | solution.py:68
  70.8 1.0 copy-start.20
  70.8 1.0 copy-start.28
  71.8 12.3 %copy-start.8 = (f32[2,2,2,128,1024]{4,3,1,0,2:T(8,128)S(1)}, f32[2,2,2,128,1024]{4,3,1,0,2:T(8,128)}, u32[]{:S(2)}) copy-start(f32[2,2,2,128,1024]{4,3,1,0,2:T(8,128)} %maximum_convert_fusion) | copy-start | bytes 12582916
  71.8 12.3 %copy-start.27 = (f32[2]{0:T(128)S(1)}, f32[2]{0:T(128)}, u32[]{:S(2)}) copy-start(f32[2]{0:T(128)} %constant.8.clone) | copy-start | bytes 28
  84.2 5.8 slice-start
  85.2 4.8 slice-start.1
  161.5 5.3 copy-start.21
  166.8 6.2 copy-start
  166.9 6.2 copy-start.18
  166.9 6.2 copy-start.19
  173.0 2.3 copy-start.2
  242.5 5.3 copy-start.22
  320.7 5.3 copy-start.23
  326.0 6.1 copy-start.4
  326.0 6.1 copy-start.17
  332.1 2.3 copy-start.6
  401.6 5.3 copy-start.24
  479.6 5.3 copy-start.25
  479.6 13.5 %copy-start.7 = (f32[2,2,2,128,1024]{4,3,2,0,1:T(8,128)S(1)}, f32[2,2,2,128,1024]{4,3,2,0,1:T(8,128)}, u32[]{:S(2)}) copy-start(f32[2,2,2,128,1024]{4,3,2,0,1:T(8,128)} %copy-done.6) | copy-start | bytes 12582916
  485.0 8.2 %copy-start.9 = (f32[2,2,2,128,1024]{4,3,2,0,1:T(8,128)}, f32[2,2,2,128,1024]{4,3,2,0,1:T(8,128)S(1)}, u32[]{:S(2)}) copy-start(f32[2,2,2,128,1024]{4,3,2,0,1:T(8,128)S(1)} %fusion.24) | copy-start | bytes 12582916
  485.0 8.2 %copy-start.1 = (f32[2,2,2,128,1024]{4,3,2,0,1:T(8,128)S(1)}, f32[2,2,2,128,1024]{4,3,2,0,1:T(8,128)}, u32[]{:S(2)}) copy-start(f32[2,2,2,128,1024]{4,3,2,0,1:T(8,128)} %copy-done) | copy-start | bytes 12582916
  485.0 8.2 %copy-start.3 = (f32[2,2,2,128,1024]{4,3,2,0,1:T(8,128)S(1)}, f32[2,2,2,128,1024]{4,3,2,0,1:T(8,128)}, u32[]{:S(2)}) copy-start(f32[2,2,2,128,1024]{4,3,2,0,1:T(8,128)} %copy-done.2) | copy-start | bytes 12582916
  485.0 8.2 %copy-start.5 = (f32[2,2,2,128,1024]{4,3,2,0,1:T(8,128)S(1)}, f32[2,2,2,128,1024]{4,3,2,0,1:T(8,128)}, u32[]{:S(2)}) copy-start(f32[2,2,2,128,1024]{4,3,2,0,1:T(8,128)} %copy-done.4) | copy-start | bytes 12582916
  499.6 6.2 copy-start.10
  499.6 6.7 copy-start.14
  499.6 6.7 copy-start.15
  505.9 1.6 copy-start.11
  505.9 2.2 copy-start.12
  505.9 2.9 copy-start.13
  505.9 2.8 copy-start.29
  511.3 34.6 %all-gather.9.cloned.1.call-start = ((), (), s32[]{:S(2)}) async-start(), calls=%async_computation.9 | async-start | bytes 1310720 | tf_op jit(solution)/shard_map/all_gather | solution.py:68
  512.1 52.2 %all-gather.11.cloned.1.call-start = ((), (), s32[]{:S(2)}) async-start(), calls=%async_computation.10 | async-start | bytes 1310720 | tf_op jit(solution)/shard_map/all_gather | solution.py:68
  569.5 31.9 %all-to-all-start.7 = ((bf16[3,8,16384]{2,0,1:T(4,128)(2,1)}), bf16[3,8,16384]{2,0,1:T(4,128)(2,1)S(1)}, u32[]{:S(2)}, u32[]{:S(2)}) async-start(bf16[3,8,16384]{2,0,1:T(4,128)(2,1)} %reshape.290), calls=%async_computation.7 | async-start | bytes 2097152 | tf_op jit(solution)/shard_map/all_to_all | solution.py:111
  575.3 1.9 copy-start.16
  601.4 52.1 %all-to-all-start.6 = ((bf16[2,2,2,8,16384]{4,2,1,0,3:T(2,128)(2,1)}), bf16[2,2,2,8,16384]{4,2,1,0,3:T(2,128)(2,1)S(1)}, u32[]{:S(2)}, u32[]{:S(2)}) async-start(bf16[2,2,2,8,16384]{4,2,1,0,3:T(2,128)(2,1)} %copy.317), calls=%async_computation.6 | async-start | bytes 4194304 | tf_op jit(solution)/shard_map/all_to_all | solution.py:101
Sparse Core Ops, SparseCore 0:
  511.5 15.6 all-gather.6
  529.3 16.6 all-gather.8
  547.5 16.6 all-gather.10
